TPU v7x, 32 devices: a whole 2x2x4 slice. The times are simulated.
32 devices in a mesh: parts: 2 (over x), seq: 16 (over z, y, core).
Axes of the slice: x: 2, y: 2, z: 4, core: 2. Of those that a mesh axis runs over, the one named last changes fastest.
Arguments:
- control: bfloat16 [256, 3072], P(('parts', 'seq')), parts along dimension 0, may hold values from -6 to 6
- mask_ids: int32 [256], P(('parts', 'seq')), parts along dimension 0, may hold values from 0 to 2
- owner: int32 [256], P('parts'), parts along dimension 0, may hold values from 0 to 127, each once
- mask_table: bfloat16 [3, 3072], replicated, may hold values from -6 to 6
- res_weight: bfloat16 [3072, 3072], P(None, 'seq'), may hold values from -0.109375 to 0.109375
- base: bfloat16 [256, 3072], P(('parts', 'seq')), parts along dimension 0, may hold values from -6 to 6
- modulation: float32 [2, 3072], replicated, may hold values from -0.5 to 0.5
- q_weight: bfloat16 [3072, 1536], P(None, 'seq'), may hold values from -1 to 1
- k_weight: bfloat16 [3072, 1536], P(None, 'seq'), may hold values from -4 to 4
- v_weight: bfloat16 [3072, 1536], P(None, 'seq'), may hold values from -0.109375 to 0.109375
Outputs:
- hidden_out: bfloat16 [256, 3072], P(('parts', 'seq')), parts along dimension 0
- attended: bfloat16 [256, 1536], P(('parts', 'seq')), parts along dimension 0
There are 2 independent parts, one for each index of `parts`. A program takes and returns all parts, laid end to end along the dimension named above; an argument that names none is the same for every part. Nothing has to cross between parts.
Inputs may be any that keep to these rules, and one draw needn't show every extreme that they name: `owner`: each base row is named by exactly one control row.
All inputs are finite; a program needn't handle non-finite values.
Results may differ from a plain program's by a relative error of at most 0.006.
Values may be sent and summed in bfloat16 or wider, within the bound.
No kernel may reach another device: no remote copies, remote signals or barrier semaphores. Data moves between devices by JAX's collectives and lax.ppermute only.
A program may use at most 64 MiB of HBM per device.

v0:
```python
import functools
import math

import jax
import jax.numpy as jnp
from jax import lax
from jax.experimental import pallas as pl
from jax.experimental.pallas import tpu as pltpu
from jax.sharding import PartitionSpec as P


HEAD_DIM = 128


def ring_order(devices):
    chips = devices // 2
    narrow = 1
    while (2 * narrow) ** 2 <= chips and chips % (2 * narrow) == 0:
        narrow *= 2
    long = chips // narrow
    if narrow == 1:
        walk = [(row, 0) for row in range(long)]
    else:
        walk = [(row, 0) for row in range(long)]
        for back, row in enumerate(reversed(range(long))):
            columns = range(1, narrow) if back % 2 == 0 else range(narrow - 1, 0, -1)
            walk += [(row, column) for column in columns]
    return [(row * narrow + column) * 2 + core for row, column in walk for core in range(2)]


def layer_norm(hidden, modulation):
    row_mean = jnp.mean(hidden, axis=1, keepdims=True)
    centred = hidden - row_mean
    row_var = jnp.mean(centred * centred, axis=1, keepdims=True)
    scaled = centred * lax.rsqrt(row_var + 1e-06)
    return (scaled * (1.0 + modulation[1]) + modulation[0]).astype(jnp.bfloat16)


def on_device_plain(
    devices,
    control,
    mask_ids,
    owner,
    mask_table,
    res_weight,
    base,
    modulation,
    q_weight,
    k_weight,
    v_weight,
):
    row_count = base.shape[0]
    total_rows = owner.shape[0]
    width = q_weight.shape[1]
    ring = ring_order(devices)
    team = math.lcm(width, HEAD_DIM) // width
    teams = devices // team
    team_heads = team * width // HEAD_DIM
    me = lax.axis_index("seq")
    place = me % team

    selector = (
        mask_ids[:, None] == jnp.arange(mask_table.shape[0], dtype=jnp.int32)[None, :]
    ).astype(jnp.bfloat16)
    condition = (
        control.astype(jnp.float32)
        + jnp.dot(selector, mask_table, preferred_element_type=jnp.float32)
    ).astype(jnp.bfloat16)
    conditions = lax.all_gather(condition, "seq", axis=0, tiled=True, axis_index_groups=[ring])
    residual = jnp.dot(conditions, res_weight, preferred_element_type=jnp.float32).astype(
        jnp.bfloat16
    )
    owner_ring = jnp.concatenate(
        [owner[place_ * row_count : (place_ + 1) * row_count] for place_ in ring]
    )
    relay = (jnp.arange(total_rows, dtype=jnp.int32)[:, None] == owner_ring[None, :]).astype(
        jnp.bfloat16
    )
    by_owner = jnp.dot(relay, residual, preferred_element_type=jnp.float32).astype(jnp.bfloat16)
    relayed = lax.all_to_all(by_owner, "seq", split_axis=0, concat_axis=1, tiled=True)
    hidden = base.astype(jnp.float32) + relayed.astype(jnp.float32)
    normed = layer_norm(hidden, modulation)
    joined = jnp.concatenate([q_weight, k_weight, v_weight], axis=1)
    normed_all = lax.all_gather(normed, "seq", axis=0, tiled=True, axis_index_groups=[ring])
    columns = lax.dot_general(
        joined, normed_all, (((0,), (1,)), ((), ())), preferred_element_type=jnp.float32
    ).astype(jnp.bfloat16)
    team_groups = [[t * team + r for r in range(team)] for t in range(teams)]
    columns = lax.all_gather(columns, "seq", axis=0, axis_index_groups=team_groups)
    columns = columns.reshape(team, 3, width, total_rows).transpose(1, 0, 2, 3)
    columns = columns.reshape(3, team_heads, HEAD_DIM, total_rows)
    spots = jnp.array([ring.index(d) for d in range(devices)], jnp.int32).reshape(teams, team)
    blocks = columns[0].reshape(team_heads, HEAD_DIM, devices, row_count)
    queries = jnp.take(blocks, jnp.take(spots, place, axis=1), axis=2)
    queries = queries.reshape(team_heads, HEAD_DIM, teams * row_count)
    scores = jnp.einsum(
        "hdt,hdk->htk", queries, columns[1], preferred_element_type=jnp.float32
    ) / math.sqrt(HEAD_DIM)
    expo = jnp.exp(scores - jnp.max(scores, axis=2, keepdims=True))
    denom = jnp.sum(expo, axis=2)
    summed = jnp.einsum(
        "htk,hdk->thd",
        expo.astype(jnp.bfloat16),
        columns[2],
        preferred_element_type=jnp.float32,
    )
    mine = (summed / denom.T[:, :, None]).astype(jnp.bfloat16)
    mine = mine.reshape(teams, row_count, team_heads * HEAD_DIM)
    place_groups = [[t * team + r for t in range(teams)] for r in range(team)]
    parts = lax.all_to_all(
        mine, "seq", split_axis=0, concat_axis=0, tiled=True, axis_index_groups=place_groups
    )
    attended = parts.transpose(1, 0, 2).reshape(row_count, teams * team_heads * HEAD_DIM)
    return (hidden.astype(jnp.bfloat16), attended)


VMEM = pl.BlockSpec(memory_space=pltpu.VMEM)
SMEM = pl.BlockSpec(memory_space=pltpu.SMEM)
HBM = pl.BlockSpec(memory_space=pltpu.HBM)
NT = (((1,), (1,)), ((), ()))
LANES = 128
GATHER_BYTES = 1 << 20


def call(kernel, out_shape, in_specs, scratch=(), limit=8 << 20):
    multiple = isinstance(out_shape, (tuple, list))
    return pl.pallas_call(
        kernel,
        out_shape=out_shape,
        in_specs=in_specs,
        out_specs=[VMEM] * len(out_shape) if multiple else VMEM,
        scratch_shapes=list(scratch),
        compiler_params=pltpu.CompilerParams(vmem_limit_bytes=limit),
    )


def matmul_nt(left, right):
    return lax.dot_general(left, right, NT, preferred_element_type=jnp.float32)


def identity(size):
    rows = lax.broadcasted_iota(jnp.int32, (size, size), 0)
    return (rows == lax.broadcasted_iota(jnp.int32, (size, size), 1)).astype(jnp.bfloat16)


def condition_kernel(
    far_ids,
    far_control,
    far_table,
    far_base,
    far_owner,
    block,
    tail,
    owner,
    ids,
    table,
    control,
    base,
    arrived,
):
    copies = [
        pltpu.make_async_copy(source, target, arrived.at[i])
        for i, (source, target) in enumerate(
            (
                (far_ids, ids),
                (far_table, table),
                (far_control, control),
                (far_base, base),
                (far_owner, owner),
            )
        )
    ]
    for copy in copies:
        copy.start()
    rows, model = control.shape
    kinds = table.shape[0]
    head = block.shape[1] - model
    copies[0].wait()
    kind = jnp.zeros((rows, 1), jnp.int32)
    row = lax.broadcasted_iota(jnp.int32, (rows, 1), 0)
    for i in range(rows):
        kind = jnp.where(row == i, ids[i], kind)
    copies[1].wait()
    copies[2].wait()
    entries = table[...].astype(jnp.float32)
    chosen = jnp.broadcast_to(entries[:1], (rows, model))
    for j in range(1, kinds):
        chosen = jnp.where(kind == j, entries[j : j + 1], chosen)
    block[:, :model] = (control[...].astype(jnp.float32) + chosen).astype(jnp.bfloat16)
    copies[3].wait()
    block[:, model:] = base[:, :head]
    for tile in range(tail.shape[0] // rows):
        lanes = slice(head + tile * LANES, head + (tile + 1) * LANES)
        tail[tile * rows : (tile + 1) * rows] = base[:, lanes]
    copies[4].wait()


def natural_rows(me, team, near, rows):
    count = near // team
    far = (rows - near) // near
    lane = lax.broadcasted_iota(jnp.int32, (1, rows), 1)
    block_at = lane // count
    beyond = block_at - team
    step = jnp.where(beyond < 0, 0, beyond % far + 1)
    member = jnp.where(beyond < 0, block_at, beyond // far)
    holder = ((me // team) ^ step) * team + member
    row = lax.broadcasted_iota(jnp.int32, (rows, rows), 0)
    return (row == holder * count + lane % count).astype(jnp.bfloat16)


def residual_kernel(team, me, own, others, weight, owner, tail, out):
    block, model = weight.shape
    near = own.shape[0]
    rows = near + others.shape[0]
    conditions = jnp.concatenate([own[:, :model], others[:, :model]], axis=0)
    residual = matmul_nt(weight[...], conditions).astype(jnp.bfloat16)
    row = lax.broadcasted_iota(jnp.int32, (rows, rows), 0)
    names = (row == owner[...]).astype(jnp.bfloat16)
    relay = jnp.dot(
        names, natural_rows(me[0], team, near, rows), preferred_element_type=jnp.float32
    ).astype(jnp.bfloat16)
    out[:block] = matmul_nt(residual, relay).astype(jnp.bfloat16)
    out[block:] = tail[...]


def fold(values):
    tiles = [values[:, i : i + LANES] for i in range(0, values.shape[1], LANES)]
    return sum(tiles[1:], tiles[0])


def project_kernel(
    ring,
    team,
    me,
    gathered,
    own,
    others,
    modulation,
    q_weight,
    k_weight,
    v_weight,
    columns,
    hidden_out,
    hidden,
    normed,
):
    devices = len(ring)
    rows, model = hidden.shape
    stride = gathered.shape[0] // devices
    block = model // devices
    count = hidden_out.shape[0]
    head = own.shape[1] - model
    turned = natural_rows(me[0], team, own.shape[0], rows)
    eye = identity(rows)
    pair = 2 * block
    spans = []
    total = jnp.zeros((rows, LANES), jnp.float32)
    squares = jnp.zeros((rows, LANES), jnp.float32)
    for p in range(devices // 2):
        first = ring[2 * p] * block
        lanes = slice(first, first + pair)
        spans.append(lanes)
        start = 2 * p * stride
        relayed = jnp.concatenate(
            [gathered[start : start + block], gathered[start + stride : start + stride + block]],
            axis=0,
        )
        if first < head:
            there = slice(model + first, model + first + pair)
            placed = jnp.dot(
                turned,
                jnp.concatenate([own[:, there], others[:, there]], axis=0),
                preferred_element_type=jnp.float32,
            )
        else:
            for tile in range(pair // LANES):
                at = first + tile * LANES
                for s, device in enumerate(ring):
                    row = s * stride + block + (at - head) // LANES * count
                    hidden[device * count : (device + 1) * count, at : at + LANES] = gathered[
                        row : row + count
                    ].astype(jnp.float32)
            placed = hidden[:, lanes]
        summed = placed + matmul_nt(eye, relayed)
        hidden[:, lanes] = summed
        if p == 0:
            near = jnp.sum(fold(summed), axis=1, keepdims=True) * (1.0 / pair)
        apart = summed - near
        total = total + fold(apart)
        squares = squares + fold(apart * apart)
    shift = jnp.sum(total, axis=1, keepdims=True) * (1.0 / model)
    mean = near + shift
    spread = jnp.sum(squares, axis=1, keepdims=True) * (1.0 / model) - shift * shift
    inverse = lax.rsqrt(spread + 1e-06)
    for lanes in spans:
        scaled = ((hidden[:, lanes] - mean) * inverse) * (1.0 + modulation[1:2, lanes])
        normed[:, lanes] = (scaled + modulation[0:1, lanes]).astype(jnp.bfloat16)
    first = pl.multiple_of(me[0] * count, count)
    hidden_out[...] = hidden[pl.ds(first, count), :].astype(jnp.bfloat16)
    weights = jnp.concatenate([q_weight[...], k_weight[...], v_weight[...]], axis=0)
    columns[...] = matmul_nt(weights, normed[...]).astype(jnp.bfloat16)


def attend_kernel(me, gathered, *refs):
    outs, (queries, keys, values) = refs[:-3], refs[-3:]
    team, tall, rows = gathered.shape
    width = tall // 3
    teams, count = len(outs), outs[0].shape[0]
    for r in range(team):
        span = slice(r * width, (r + 1) * width)
        queries[span] = gathered[r, :width]
        keys[span] = gathered[r, width : 2 * width]
        values[span] = gathered[r, 2 * width :]
    line = lax.broadcasted_iota(jnp.int32, (teams * count, rows), 0)
    wanted = (((me[0] // team) ^ (line // count)) * team + me[0] % team) * count + line % count
    pick = (wanted == lax.broadcasted_iota(jnp.int32, (teams * count, rows), 1)).astype(
        jnp.bfloat16
    )
    chosen = matmul_nt(pick, queries[...]).astype(jnp.bfloat16)
    for h in range(team * width // HEAD_DIM):
        span = slice(h * HEAD_DIM, (h + 1) * HEAD_DIM)
        scores = jnp.dot(
            chosen[:, span], keys[span], preferred_element_type=jnp.float32
        ) / math.sqrt(HEAD_DIM)
        expo = jnp.exp(scores - jnp.max(scores, axis=1, keepdims=True))
        denom = jnp.sum(expo, axis=1, keepdims=True)
        mixed = matmul_nt(expo.astype(jnp.bfloat16), values[span]) / denom
        for k, out in enumerate(outs):
            out[:, span] = mixed[k * count : (k + 1) * count].astype(jnp.bfloat16)


def gather_kernel(team, me, *refs):
    blocks, out = refs[:-1], refs[-1]
    columns = blocks[0].shape[1]
    for k, block in enumerate(blocks):
        first = pl.multiple_of(((me[0] // team) ^ k) * columns, columns)
        out[:, pl.ds(first, columns)] = block[...]


def on_device(
    devices,
    control,
    mask_ids,
    owner,
    mask_table,
    res_weight,
    base,
    modulation,
    q_weight,
    k_weight,
    v_weight,
):
    count, model = base.shape
    rows = owner.shape[0]
    block = res_weight.shape[1]
    width = q_weight.shape[1]
    ring = ring_order(devices)
    team = math.lcm(width, HEAD_DIM) // width
    teams = devices // team
    me = lax.axis_index("seq")
    bf16 = jnp.bfloat16
    shape = jax.ShapeDtypeStruct

    tiles = ((GATHER_BYTES - 1) // (2 * devices * rows) - block) // count
    tiles -= tiles % (2 * block // LANES)
    head = model - tiles * LANES

    inputs = (mask_ids, control, mask_table, base, owner.reshape(1, rows))
    mine, tail, near_owner = call(
        condition_kernel,
        (
            pltpu.VMEM((count, model + head), bf16),
            pltpu.VMEM((tiles * count, LANES), bf16),
            pltpu.VMEM((1, rows), jnp.int32),
        ),
        [HBM] * len(inputs),
        [
            pltpu.SMEM((count,), jnp.int32),
            pltpu.VMEM(mask_table.shape, bf16),
            pltpu.VMEM((count, model), bf16),
            pltpu.VMEM((count, model), bf16),
            pltpu.SemaphoreType.DMA((len(inputs),)),
        ],
    )(*[pltpu.with_memory_space_constraint(x, pltpu.HBM) for x in inputs])
    team_groups = [[t * team + r for r in range(team)] for t in range(teams)]
    sent = [
        lax.ppermute(mine, "seq", [(d, d ^ (k * team)) for d in range(devices)])
        for k in range(1, teams)
    ]
    own = lax.all_gather(mine, "seq", axis=0, tiled=True, axis_index_groups=team_groups)
    others = lax.all_gather(
        jnp.concatenate(sent, axis=0), "seq", axis=0, tiled=True, axis_index_groups=team_groups
    )
    payload = call(
        functools.partial(residual_kernel, team),
        shape((block + tiles * count, rows), bf16),
        [SMEM] + [VMEM] * 5,
    )(me.reshape(1), own, others, res_weight.T, near_owner, tail)
    gathered = lax.all_gather(payload, "seq", axis=0, tiled=True, axis_index_groups=[ring])
    columns, hidden_out = call(
        functools.partial(project_kernel, ring, team),
        (shape((3 * width, rows), bf16), shape((count, model), bf16)),
        [SMEM] + [VMEM] * 7,
        [pltpu.VMEM((rows, model), jnp.float32), pltpu.VMEM((rows, model), bf16)],
    )(me.reshape(1), gathered, own, others, modulation, q_weight.T, k_weight.T, v_weight.T)
    columns = lax.all_gather(columns, "seq", axis=0, axis_index_groups=team_groups)
    head_columns = team * width
    results = call(
        attend_kernel,
        tuple(shape((count, head_columns), bf16) for _ in range(teams)),
        [SMEM, VMEM],
        [pltpu.VMEM((head_columns, rows), bf16)] * 3,
    )(me.reshape(1), columns)
    crossed = {}
    for k in range(1, teams):
        crossed[k] = lax.ppermute(results[k], "seq", [(d, d ^ (k * team)) for d in range(devices)])
    parts = [results[0]] + [crossed[k] for k in range(1, teams)]
    attended = call(
        functools.partial(gather_kernel, team),
        shape((count, teams * head_columns), bf16),
        [SMEM] + [VMEM] * teams,
    )(me.reshape(1), *parts)
    return (hidden_out, attended)


def fits(devices, rows, block, width):
    team = math.lcm(width, HEAD_DIM) // width
    powers = all(n & (n - 1) == 0 for n in (devices, team))
    return rows == LANES and devices > team > 1 and powers and block % 64 == 0 and width % 16 == 0


def on_any_device(devices, *arguments):
    owner, res_weight, q_weight = arguments[2], arguments[4], arguments[7]
    tidy = fits(devices, owner.shape[0], res_weight.shape[1], q_weight.shape[1])
    return (on_device if tidy else on_device_plain)(devices, *arguments)


def solution(mesh):
    in_specs = (
        P(("parts", "seq"), None),
        P(("parts", "seq")),
        P("parts"),
        P(),
        P(None, "seq"),
        P(("parts", "seq"), None),
        P(),
        P(None, "seq"),
        P(None, "seq"),
        P(None, "seq"),
    )
    out_specs = (P(("parts", "seq"), None), P(("parts", "seq"), None))
    return jax.shard_map(
        functools.partial(on_any_device, mesh.shape["seq"]),
        mesh=mesh,
        in_specs=in_specs,
        out_specs=out_specs,
        check_vma=False,
    )
```

profile of v0, /device:TPU:0, one launch (start us, length us, event | category | flops | bytes accessed | tf_op | source)
XLA Modules:
  0.0 58.9 jit_solution(3638313765173448759)
XLA Ops:
  0.6 1.0 %shard_map.113 = (bf16[8,5376]{1,0:T(8,128)(2,1)S(1)}, bf16[48,128]{1,0:T(8,128)(2,1)S(1)}, s32[1,128]{1,0:T(1,128)S(1)}) custom-call(s32[8]{0:T(128)} %far_ids.1, bf16[8,3072]{1,0:T(8,128)(2,1)} %far_control.1, bf16[3,3072]{1,0:T(4,128)(2,1)} %far_table.1, bf16[8,3072]{1,0:T(8,128)(2,1)} %far_base.1, s32[1,128]{1,0:T(1,128)} %bitcast.12), custom_call_target="tpu_custom_call" | custom-call | tf_op jit(solution)/shard_map/pallas_call | solution.py:369
  1.6 5.1 %collective-permute-start.2 = (bf16[8,5376]{1,0:T(8,128)(2,1)S(1)}, bf16[8,5376]{1,0:T(8,128)(2,1)S(1)}, u32[]{:S(2)}, u32[]{:S(2)}) collective-permute-start(bf16[8,5376]{1,0:T(8,128)(2,1)S(1)} %get-tuple-element.11), channel_id=1, source_target_pairs={{0,12},{1,13},{2,14},{3,15},{4,8},{5,9},{6,10},{7,11},{8,4},{9,5},... | collective-permute-start | bytes 258056 | tf_op jit(solution)/shard_map/ppermute | solution.py:387
  6.8 0.0 collective-permute-start.1
  6.8 0.6 %collective-permute-start = (bf16[8,5376]{1,0:T(8,128)(2,1)S(1)}, bf16[8,5376]{1,0:T(8,128)(2,1)S(1)}, u32[]{:S(2)}, u32[]{:S(2)}) collective-permute-start(bf16[8,5376]{1,0:T(8,128)(2,1)S(1)} %get-tuple-element.11), channel_id=1, source_target_pairs={{0,4},{1,5},{2,6},{3,7},{4,0},{5,1},{6,2},{7,3},{8,12},{9,13},{10,... | collective-permute-start | bytes 258056 | tf_op jit(solution)/shard_map/ppermute | solution.py:387
  7.4 6.3 %all_gather.15.own = bf16[32,5376]{1,0:T(8,128)(2,1)S(1)} all-gather(bf16[8,5376]{1,0:T(8,128)(2,1)S(1)} %get-tuple-element.11), channel_id=1, replica_groups={{0,1,2,3},{4,5,6,7},{8,9,10,11},{12,13,14,15},{16,17,18,19},{20,21,22,2..., dimensions={0}, use_global_device_ids=true | all-gather | bytes 430080 | tf_op jit(solution)/shard_map/all_gather | solution.py:390
  13.8 0.0 collective-permute-done.2
  13.8 0.2 collective-permute-done.1
  14.0 0.0 collective-permute-done
  14.0 10.0 %all_gather.16.others = bf16[96,5376]{1,0:T(8,128)(2,1)S(1)} all-gather(bf16[24,5376]{1,0:T(8,128)(2,1)S(1)} %pad_maximum_fusion), channel_id=1, replica_groups={{0,1,2,3},{4,5,6,7},{8,9,10,11},{12,13,14,15},{16,17,18,19},{20,21,22,2..., dimensions={0}, use_global_device_ids=true | all-gather | bytes 1290240 | tf_op jit(solution)/shard_map/all_gather | solution.py:391
  24.0 0.0 copy-done
  24.0 0.6 %shard_map.114 = bf16[240,128]{1,0:T(8,128)(2,1)S(1)} custom-call(s32[1]{0:T(128)} %bitcast.me, bf16[32,5376]{1,0:T(8,128)(2,1)S(1)} %all_gather.15.own, bf16[96,5376]{1,0:T(8,128)(2,1)S(1)} %all_gather.16.others, bf16[192,3072]{1,0:T(8,128)(2,1)S(1)} %bitcast.7, s32[1,128]{1,0:T(1,128)S(1)} %get-tuple-element.12.owner, ...), custom_call_target="tpu_custom_call" | custom-call | tf_op jit(solution)/shard_map/pallas_call | solution.py:394
  24.6 0.0 copy-start.1
  24.7 17.1 %all_gather.17.gathered = bf16[3840,128]{1,0:T(8,128)(2,1)S(1)} all-gather(bf16[240,128]{1,0:T(8,128)(2,1)S(1)} %shard_map.114), channel_id=1, replica_groups={{0,1,4,5,8,9,12,13,14,15,10,11,6,7,2,3},{16,17,20,21,24,25,28,29,30,31,..., dimensions={0}, use_global_device_ids=true | all-gather | bytes 1044480 | tf_op jit(solution)/shard_map/all_gather | solution.py:399
  41.8 0.0 copy-done.3
  41.8 1.4 %shard_map.115 = (bf16[288,128]{1,0:T(8,128)(2,1)S(1)}, bf16[8,3072]{1,0:T(8,128)(2,1)}) custom-call(s32[1]{0:T(128)} %bitcast.me, bf16[3840,128]{1,0:T(8,128)(2,1)S(1)} %all_gather.17.gathered, bf16[32,5376]{1,0:T(8,128)(2,1)S(1)} %all_gather.15.own, bf16[96,5376]{1,0:T(8,128)(2,1)S(1)} %all_gather.16.others, f32[2,3072]{1,0:T(2,128)S(1)} %copy-done.4, ...), custom_call_target="tpu_custom_call" | custom-call | tf_op jit(solution)/shard_map/pallas_call | solution.py:400
  43.3 6.0 %all-gather = bf16[1152,128]{1,0:T(8,128)(2,1)S(1)} all-gather(bf16[288,128]{1,0:T(8,128)(2,1)S(1)} %get-tuple-element.15), channel_id=2, replica_groups={{0,1,2,3},{4,5,6,7},{8,9,10,11},{12,13,14,15},{16,17,18,19},{20,21,22,2..., dimensions={0}, use_global_device_ids=true | all-gather | bytes 368640 | tf_op jit(solution)/shard_map/all_gather | solution.py:406
  49.3 0.7 %shard_map.116 = (bf16[8,384]{1,0:T(8,128)(2,1)S(1)}, bf16[8,384]{1,0:T(8,128)(2,1)S(1)}, bf16[8,384]{1,0:T(8,128)(2,1)S(1)}, bf16[8,384]{1,0:T(8,128)(2,1)S(1)}) custom-call(s32[1]{0:T(128)} %bitcast.me, bf16[4,288,128]{2,1,0:T(8,128)(2,1)S(1)} %bitcast.8), custom_call_target="tpu_custom_call" | custom-call | tf_op jit(solution)/shard_map/pallas_call | solution.py:408
  50.0 1.4 %collective-permute-start.3 = (bf16[8,384]{1,0:T(8,128)(2,1)S(1)}, bf16[8,384]{1,0:T(8,128)(2,1)S(1)}, u32[]{:S(2)}, u32[]{:S(2)}) collective-permute-start(bf16[8,384]{1,0:T(8,128)(2,1)S(1)} %get-tuple-element.17), channel_id=1, source_target_pairs={{0,4},{1,5},{2,6},{3,7},{4,0},{5,1},{6,2},{7,3},{8,12},{9,13},{10,... | collective-permute-start | bytes 18440 | tf_op jit(solution)/shard_map/ppermute | solution.py:416
  51.4 1.5 %collective-permute-start.4 = (bf16[8,384]{1,0:T(8,128)(2,1)S(1)}, bf16[8,384]{1,0:T(8,128)(2,1)S(1)}, u32[]{:S(2)}, u32[]{:S(2)}) collective-permute-start(bf16[8,384]{1,0:T(8,128)(2,1)S(1)} %get-tuple-element.18), channel_id=1, source_target_pairs={{0,8},{1,9},{2,10},{3,11},{4,12},{5,13},{6,14},{7,15},{8,0},{9,1},... | collective-permute-start | bytes 18440 | tf_op jit(solution)/shard_map/ppermute | solution.py:416
  52.8 1.6 %collective-permute-start.5 = (bf16[8,384]{1,0:T(8,128)(2,1)S(1)}, bf16[8,384]{1,0:T(8,128)(2,1)S(1)}, u32[]{:S(2)}, u32[]{:S(2)}) collective-permute-start(bf16[8,384]{1,0:T(8,128)(2,1)S(1)} %get-tuple-element.19), channel_id=1, source_target_pairs={{0,12},{1,13},{2,14},{3,15},{4,8},{5,9},{6,10},{7,11},{8,4},{9,5},... | collective-permute-start | bytes 18440 | tf_op jit(solution)/shard_map/ppermute | solution.py:416
  54.4 0.0 collective-permute-done.3.refs_1_
  54.4 1.5 %collective-permute-done.4.refs_2_ = bf16[8,384]{1,0:T(8,128)(2,1)S(1)} collective-permute-done((bf16[8,384]{1,0:T(8,128)(2,1)S(1)}, bf16[8,384]{1,0:T(8,128)(2,1)S(1)}, u32[]{:S(2)}, u32[]{:S(2)}) %collective-permute-start.4) | collective-permute-done | bytes 6176 | tf_op jit(solution)/shard_map/ppermute | solution.py:416
  55.9 2.4 %collective-permute-done.5.refs_3_ = bf16[8,384]{1,0:T(8,128)(2,1)S(1)} collective-permute-done((bf16[8,384]{1,0:T(8,128)(2,1)S(1)}, bf16[8,384]{1,0:T(8,128)(2,1)S(1)}, u32[]{:S(2)}, u32[]{:S(2)}) %collective-permute-start.5) | collective-permute-done | bytes 6176 | tf_op jit(solution)/shard_map/ppermute | solution.py:416
  58.3 0.6 %shard_map.117 = bf16[8,1536]{1,0:T(8,128)(2,1)} custom-call(s32[1]{0:T(128)} %bitcast.me, bf16[8,384]{1,0:T(8,128)(2,1)S(1)} %get-tuple-element.16.refs_0_, bf16[8,384]{1,0:T(8,128)(2,1)S(1)} %collective-permute-done.3.refs_1_, bf16[8,384]{1,0:T(8,128)(2,1)S(1)} %collective-permute-done.4.refs_2_, bf16[8,384]{1,0:T(8,128)(2,1)S(1)} %collective-permute-done.5.refs_3_), custom_call_target="tpu_custom_call" | custom-call | tf_op jit(solution)/shard_map/pallas_call | solution.py:418
  (8 shorter events, 0.0 us)
Async XLA Ops:
  0.6 23.4 %copy-start = (bf16[3072,192]{0,1:T(8,128)(2,1)S(1)}, bf16[3072,192]{0,1:T(8,128)(2,1)}, u32[]{:S(2)}) copy-start(bf16[3072,192]{0,1:T(8,128)(2,1)} %param.14) | copy-start | bytes 3538948
  1.6 12.1 %collective-permute-start.2 = (bf16[8,5376]{1,0:T(8,128)(2,1)S(1)}, bf16[8,5376]{1,0:T(8,128)(2,1)S(1)}, u32[]{:S(2)}, u32[]{:S(2)}) collective-permute-start(bf16[8,5376]{1,0:T(8,128)(2,1)S(1)} %get-tuple-element.11), channel_id=1, source_target_pairs={{0,12},{1,13},{2,14},{3,15},{4,8},{5,9},{6,10},{7,11},{8,4},{9,5},... | collective-permute-start | bytes 258056 | tf_op jit(solution)/shard_map/ppermute | solution.py:387
  6.8 7.2 %collective-permute-start.1 = (bf16[8,5376]{1,0:T(8,128)(2,1)S(1)}, bf16[8,5376]{1,0:T(8,128)(2,1)S(1)}, u32[]{:S(2)}, u32[]{:S(2)}) collective-permute-start(bf16[8,5376]{1,0:T(8,128)(2,1)S(1)} %get-tuple-element.11), channel_id=1, source_target_pairs={{0,8},{1,9},{2,10},{3,11},{4,12},{5,13},{6,14},{7,15},{8,0},{9,1},... | collective-permute-start | bytes 258056 | tf_op jit(solution)/shard_map/ppermute | solution.py:387
  6.8 7.2 %collective-permute-start = (bf16[8,5376]{1,0:T(8,128)(2,1)S(1)}, bf16[8,5376]{1,0:T(8,128)(2,1)S(1)}, u32[]{:S(2)}, u32[]{:S(2)}) collective-permute-start(bf16[8,5376]{1,0:T(8,128)(2,1)S(1)} %get-tuple-element.11), channel_id=1, source_target_pairs={{0,4},{1,5},{2,6},{3,7},{4,0},{5,1},{6,2},{7,3},{8,12},{9,13},{10,... | collective-permute-start | bytes 258056 | tf_op jit(solution)/shard_map/ppermute | solution.py:387
  24.0 17.8 %copy-start.2 = (bf16[3072,96]{0,1:T(8,128)(2,1)S(1)}, bf16[3072,96]{0,1:T(8,128)(2,1)}, u32[]{:S(2)}) copy-start(bf16[3072,96]{0,1:T(8,128)(2,1)} %param.18) | copy-start | bytes 1769476
  24.0 17.8 %copy-start.3 = (bf16[3072,96]{0,1:T(8,128)(2,1)S(1)}, bf16[3072,96]{0,1:T(8,128)(2,1)}, u32[]{:S(2)}) copy-start(bf16[3072,96]{0,1:T(8,128)(2,1)} %param.19) | copy-start | bytes 1769476
  24.0 17.8 %copy-start.4 = (f32[2,3072]{1,0:T(2,128)S(1)}, f32[2,3072]{1,0:T(2,128)}, u32[]{:S(2)}) copy-start(f32[2,3072]{1,0:T(2,128)} %modulation.1) | copy-start | bytes 73732
  24.6 17.2 %copy-start.1 = (bf16[3072,96]{0,1:T(8,128)(2,1)S(1)}, bf16[3072,96]{0,1:T(8,128)(2,1)}, u32[]{:S(2)}) copy-start(bf16[3072,96]{0,1:T(8,128)(2,1)} %param.17) | copy-start | bytes 1769476
  50.0 4.4 %collective-permute-start.3 = (bf16[8,384]{1,0:T(8,128)(2,1)S(1)}, bf16[8,384]{1,0:T(8,128)(2,1)S(1)}, u32[]{:S(2)}, u32[]{:S(2)}) collective-permute-start(bf16[8,384]{1,0:T(8,128)(2,1)S(1)} %get-tuple-element.17), channel_id=1, source_target_pairs={{0,4},{1,5},{2,6},{3,7},{4,0},{5,1},{6,2},{7,3},{8,12},{9,13},{10,... | collective-permute-start | bytes 18440 | tf_op jit(solution)/shard_map/ppermute | solution.py:416
  51.4 4.5 %collective-permute-start.4 = (bf16[8,384]{1,0:T(8,128)(2,1)S(1)}, bf16[8,384]{1,0:T(8,128)(2,1)S(1)}, u32[]{:S(2)}, u32[]{:S(2)}) collective-permute-start(bf16[8,384]{1,0:T(8,128)(2,1)S(1)} %get-tuple-element.18), channel_id=1, source_target_pairs={{0,8},{1,9},{2,10},{3,11},{4,12},{5,13},{6,14},{7,15},{8,0},{9,1},... | collective-permute-start | bytes 18440 | tf_op jit(solution)/shard_map/ppermute | solution.py:416
  52.8 5.4 %collective-permute-start.5 = (bf16[8,384]{1,0:T(8,128)(2,1)S(1)}, bf16[8,384]{1,0:T(8,128)(2,1)S(1)}, u32[]{:S(2)}, u32[]{:S(2)}) collective-permute-start(bf16[8,384]{1,0:T(8,128)(2,1)S(1)} %get-tuple-element.19), channel_id=1, source_target_pairs={{0,12},{1,13},{2,14},{3,15},{4,8},{5,9},{6,10},{7,11},{8,4},{9,5},... | collective-permute-start | bytes 18440 | tf_op jit(solution)/shard_map/ppermute | solution.py:416
where the time goes:
time: 59.1 us; the launch traced here: 58.9 us
  blocking collectives  39.5 us (67%)
  starting transfers between devices  10.2 us (17%)
  Pallas kernels  4.39 us (7%)
  waiting for transfers between devices  4.04 us (7%)
  between operations  0.69 us (1%)
    all_gather x1, blocking collectives, on_device(): lax.all_gather(payload, 'seq', axis=0, tiled=True, axis_index_groups=[ring])  17.1 us
    all_gather x1, blocking collectives, on_device(): lax.all_gather(jnp.concatenate(sent, axis=0), 'seq', axis=0, tiled=True,...  9.96 us
    all_gather x1, blocking collectives, on_device(): lax.all_gather(mine, 'seq', axis=0, tiled=True, axis_index_groups=team_gr...  6.35 us
    all_gather x1, blocking collectives, on_device(): lax.all_gather(columns, 'seq', axis=0, axis_index_groups=team_groups)  6.04 us
    ppermute x3, starting transfers between devices, on_device(): lax.ppermute(mine, 'seq', [(d, d ^ k * team) for d in range(devices)])  5.78 us
    ppermute x3, starting transfers between devices, on_device(): lax.ppermute(results[k], 'seq', [(d, d ^ k * team) for d in range(devices)])  4.43 us
    ppermute x3, waiting for transfers between devices, on_device(): lax.ppermute(results[k], 'seq', [(d, d ^ k * team) for d in range(devices)])  3.82 us
    pallas_call x1, Pallas kernels, on_device(): call(functools.partial(project_kernel, ring, team), (shape((3 * width, ro...  1.44 us
  transfers between devices with their start and end apart: 6, of which 3 were waited for; matrix products, arithmetic and copies ran while one was open for 0% of the time, Pallas kernels for 0%

commit v1 on v0

--- a/solution.py
+++ b/solution.py
@@ -195,29 +195,34 @@
     copies[4].wait()
 
 
-def natural_rows(me, team, near, rows):
-    count = near // team
-    far = (rows - near) // near
+def natural_rows(me, team, count, rows):
+    far = rows // (team * count) - 1
     lane = lax.broadcasted_iota(jnp.int32, (1, rows), 1)
     block_at = lane // count
     beyond = block_at - team
     step = jnp.where(beyond < 0, 0, beyond % far + 1)
-    member = jnp.where(beyond < 0, block_at, beyond // far)
+    member = jnp.where(beyond < 0, block_at ^ (me % team), beyond // far)
     holder = ((me // team) ^ step) * team + member
     row = lax.broadcasted_iota(jnp.int32, (rows, rows), 0)
     return (row == holder * count + lane % count).astype(jnp.bfloat16)
 
 
-def residual_kernel(team, me, own, others, weight, owner, tail, out):
+def stack(blocks, columns):
+    return jnp.concatenate([block[:, columns] for block in blocks], axis=0)
+
+
+def residual_kernel(team, me, *refs):
+    blocks, (weight, owner, tail, out) = refs[:-4], refs[-4:]
     block, model = weight.shape
-    near = own.shape[0]
-    rows = near + others.shape[0]
-    conditions = jnp.concatenate([own[:, :model], others[:, :model]], axis=0)
+    rows = owner.shape[1]
+    conditions = stack(blocks, slice(model))
     residual = matmul_nt(weight[...], conditions).astype(jnp.bfloat16)
     row = lax.broadcasted_iota(jnp.int32, (rows, rows), 0)
     names = (row == owner[...]).astype(jnp.bfloat16)
     relay = jnp.dot(
-        names, natural_rows(me[0], team, near, rows), preferred_element_type=jnp.float32
+        names,
+        natural_rows(me[0], team, blocks[0].shape[0], rows),
+        preferred_element_type=jnp.float32,
     ).astype(jnp.bfloat16)
     out[:block] = matmul_nt(residual, relay).astype(jnp.bfloat16)
     out[block:] = tail[...]
@@ -233,24 +238,18 @@
     team,
     me,
     gathered,
-    own,
-    others,
-    modulation,
-    q_weight,
-    k_weight,
-    v_weight,
-    columns,
-    hidden_out,
-    hidden,
-    normed,
+    *refs,
 ):
+    blocks = refs[: team + 1]
+    modulation, q_weight, k_weight, v_weight = refs[team + 1 : team + 5]
+    columns, hidden_out, hidden, normed = refs[team + 5 :]
     devices = len(ring)
     rows, model = hidden.shape
     stride = gathered.shape[0] // devices
     block = model // devices
     count = hidden_out.shape[0]
-    head = own.shape[1] - model
-    turned = natural_rows(me[0], team, own.shape[0], rows)
+    head = blocks[0].shape[1] - model
+    turned = natural_rows(me[0], team, count, rows)
     eye = identity(rows)
     pair = 2 * block
     spans = []
@@ -269,7 +268,7 @@
             there = slice(model + first, model + first + pair)
             placed = jnp.dot(
                 turned,
-                jnp.concatenate([own[:, there], others[:, there]], axis=0),
+                stack(blocks, there),
                 preferred_element_type=jnp.float32,
             )
         else:
@@ -337,6 +336,10 @@
         out[:, pl.ds(first, columns)] = block[...]
 
 
+def exchange(values, devices, step):
+    return lax.ppermute(values, "seq", [(d, d ^ step) for d in range(devices)])
+
+
 def on_device(
     devices,
     control,
@@ -383,26 +386,27 @@
         ],
     )(*[pltpu.with_memory_space_constraint(x, pltpu.HBM) for x in inputs])
     team_groups = [[t * team + r for r in range(team)] for t in range(teams)]
-    sent = [
-        lax.ppermute(mine, "seq", [(d, d ^ (k * team)) for d in range(devices)])
-        for k in range(1, teams)
-    ]
-    own = lax.all_gather(mine, "seq", axis=0, tiled=True, axis_index_groups=team_groups)
+    sent, near = [], [mine]
+    for k in range(1, teams):
+        sent.append(exchange(mine, devices, k * team))
+    for k in range(1, team):
+        near.append(exchange(mine, devices, k))
     others = lax.all_gather(
         jnp.concatenate(sent, axis=0), "seq", axis=0, tiled=True, axis_index_groups=team_groups
     )
+    blocks = near + [others]
     payload = call(
         functools.partial(residual_kernel, team),
         shape((block + tiles * count, rows), bf16),
-        [SMEM] + [VMEM] * 5,
-    )(me.reshape(1), own, others, res_weight.T, near_owner, tail)
+        [SMEM] + [VMEM] * (len(blocks) + 3),
+    )(me.reshape(1), *blocks, res_weight.T, near_owner, tail)
     gathered = lax.all_gather(payload, "seq", axis=0, tiled=True, axis_index_groups=[ring])
     columns, hidden_out = call(
         functools.partial(project_kernel, ring, team),
         (shape((3 * width, rows), bf16), shape((count, model), bf16)),
-        [SMEM] + [VMEM] * 7,
+        [SMEM] + [VMEM] * (len(blocks) + 5),
         [pltpu.VMEM((rows, model), jnp.float32), pltpu.VMEM((rows, model), bf16)],
-    )(me.reshape(1), gathered, own, others, modulation, q_weight.T, k_weight.T, v_weight.T)
+    )(me.reshape(1), gathered, *blocks, modulation, q_weight.T, k_weight.T, v_weight.T)
     columns = lax.all_gather(columns, "seq", axis=0, axis_index_groups=team_groups)
     head_columns = team * width
     results = call(
@@ -413,7 +417,7 @@
     )(me.reshape(1), columns)
     crossed = {}
     for k in range(1, teams):
-        crossed[k] = lax.ppermute(results[k], "seq", [(d, d ^ (k * team)) for d in range(devices)])
+        crossed[k] = exchange(results[k], devices, k * team)
     parts = [results[0]] + [crossed[k] for k in range(1, teams)]
     attended = call(
         functools.partial(gather_kernel, team),

time: 59.1 us -> 57.5 us (0.973)
  blocking collectives: 39.5 us -> 32.3 us
  waiting for transfers between devices: 4.04 us -> 7.89 us
  starting transfers between devices: 10.2 us -> 11.9 us
    all_gather x1 -> x0, blocking collectives: 6.35 us -> none  [on_device(): lax.all_gather(mine, 'seq', axis=0, tiled=True, axis_index_groups=team_gr...]
    ppermute x6 -> x9, waiting for transfers between devices: 4.04 us -> 7.89 us  [exchange(): return lax.ppermute(values, 'seq', [(d, d ^ step) for d in range(devices)])]
    ppermute x6 -> x9, starting transfers between devices: 10.2 us -> 11.9 us  [exchange(): return lax.ppermute(values, 'seq', [(d, d ^ step) for d in range(devices)])]
    all_gather x1, blocking collectives: 17.1 us -> 16.3 us  [on_device(): lax.all_gather(payload, 'seq', axis=0, tiled=True, axis_index_groups=[ring])]
  transfers between devices with their start and end apart: 6 -> 9, of which waited for: 3 -> 4; matrix products, arithmetic and copies ran while one was open for 0% -> 0% of each run, Pallas kernels for 0% -> 0%
where the time goes in v1:
time: 57.5 us; the launch traced here: 57.3 us
  blocking collectives  32.3 us (56%)
  starting transfers between devices  11.9 us (21%)
  waiting for transfers between devices  7.89 us (14%)
  Pallas kernels  4.43 us (8%)
  between operations  0.73 us (1%)
    all_gather x1, blocking collectives, on_device(): lax.all_gather(payload, 'seq', axis=0, tiled=True, axis_index_groups=[ring])  16.3 us
    ppermute x9, starting transfers between devices, exchange(): return lax.ppermute(values, 'seq', [(d, d ^ step) for d in range(devices)])  11.9 us
    all_gather x1, blocking collectives, on_device(): lax.all_gather(jnp.concatenate(sent, axis=0), 'seq', axis=0, tiled=True,...  9.96 us
    ppermute x9, waiting for transfers between devices, exchange(): return lax.ppermute(values, 'seq', [(d, d ^ step) for d in range(devices)])  7.89 us
    all_gather x1, blocking collectives, on_device(): lax.all_gather(columns, 'seq', axis=0, axis_index_groups=team_groups)  6.04 us
    pallas_call x1, Pallas kernels, on_device(): call(functools.partial(project_kernel, ring, team), (shape((3 * width, ro...  1.48 us
  transfers between devices with their start and end apart: 9, of which 4 were waited for; matrix products, arithmetic and copies ran while one was open for 0% of the time, Pallas kernels for 0%

profile of v1, /device:TPU:0, one launch (start us, length us, event | category | flops | bytes accessed | tf_op | source)
XLA Modules:
  0.0 57.3 jit_solution(2310395277818546359)
XLA Ops:
  0.6 1.0 %shard_map.113 = (bf16[8,5376]{1,0:T(8,128)(2,1)S(1)}, bf16[48,128]{1,0:T(8,128)(2,1)S(1)}, s32[1,128]{1,0:T(1,128)S(1)}) custom-call(s32[8]{0:T(128)} %far_ids.1, bf16[8,3072]{1,0:T(8,128)(2,1)} %far_control.1, bf16[3,3072]{1,0:T(4,128)(2,1)} %far_table.1, bf16[8,3072]{1,0:T(8,128)(2,1)} %far_base.1, s32[1,128]{1,0:T(1,128)} %bitcast.12), custom_call_target="tpu_custom_call" | custom-call | tf_op jit(solution)/shard_map/pallas_call | solution.py:372
  1.6 5.1 %collective-permute-start.5 = (bf16[8,5376]{1,0:T(8,128)(2,1)S(1)}, bf16[8,5376]{1,0:T(8,128)(2,1)S(1)}, u32[]{:S(2)}, u32[]{:S(2)}) collective-permute-start(bf16[8,5376]{1,0:T(8,128)(2,1)S(1)} %get-tuple-element.11.refs_0_), channel_id=1, source_target_pairs={{0,12},{1,13},{2,14},{3,15},{4,8},{5,9},{6,10},{7,11},{8,4},{9,5},... | collective-permute-start | bytes 258056 | tf_op jit(solution)/shard_map/ppermute | solution.py:340
  6.8 0.6 %collective-permute-start.3 = (bf16[8,5376]{1,0:T(8,128)(2,1)S(1)}, bf16[8,5376]{1,0:T(8,128)(2,1)S(1)}, u32[]{:S(2)}, u32[]{:S(2)}) collective-permute-start(bf16[8,5376]{1,0:T(8,128)(2,1)S(1)} %get-tuple-element.11.refs_0_), channel_id=1, source_target_pairs={{0,4},{1,5},{2,6},{3,7},{4,0},{5,1},{6,2},{7,3},{8,12},{9,13},{10,... | collective-permute-start | bytes 258056 | tf_op jit(solution)/shard_map/ppermute | solution.py:340
  7.4 0.4 collective-permute-start.2
  7.8 1.3 %collective-permute-start.1 = (bf16[8,5376]{1,0:T(8,128)(2,1)S(1)}, bf16[8,5376]{1,0:T(8,128)(2,1)S(1)}, u32[]{:S(2)}, u32[]{:S(2)}) collective-permute-start(bf16[8,5376]{1,0:T(8,128)(2,1)S(1)} %get-tuple-element.11.refs_0_), channel_id=1, source_target_pairs={{0,2},{1,3},{2,0},{3,1},{4,6},{5,7},{6,4},{7,5},{8,10},{9,11},{10,... | collective-permute-start | bytes 258056 | tf_op jit(solution)/shard_map/ppermute | solution.py:340
  9.1 0.9 %collective-permute-done.5 = bf16[8,5376]{1,0:T(8,128)(2,1)S(1)} collective-permute-done((bf16[8,5376]{1,0:T(8,128)(2,1)S(1)}, bf16[8,5376]{1,0:T(8,128)(2,1)S(1)}, u32[]{:S(2)}, u32[]{:S(2)}) %collective-permute-start.5) | collective-permute-done | bytes 86048 | tf_op jit(solution)/shard_map/ppermute | solution.py:340
  10.0 0.0 collective-permute-start
  10.0 4.0 %collective-permute-done.4 = bf16[8,5376]{1,0:T(8,128)(2,1)S(1)} collective-permute-done((bf16[8,5376]{1,0:T(8,128)(2,1)S(1)}, bf16[8,5376]{1,0:T(8,128)(2,1)S(1)}, u32[]{:S(2)}, u32[]{:S(2)}) %collective-permute-start.4) | collective-permute-done | bytes 86048 | tf_op jit(solution)/shard_map/ppermute | solution.py:340
  14.0 10.0 %all_gather.12.refs_4_ = bf16[96,5376]{1,0:T(8,128)(2,1)S(1)} all-gather(bf16[24,5376]{1,0:T(8,128)(2,1)S(1)} %pad_maximum_fusion), channel_id=1, replica_groups={{0,1,2,3},{4,5,6,7},{8,9,10,11},{12,13,14,15},{16,17,18,19},{20,21,22,2..., dimensions={0}, use_global_device_ids=true | all-gather | bytes 1290240 | tf_op jit(solution)/shard_map/all_gather | solution.py:394
  24.0 0.0 copy-start.2
  24.0 0.0 copy-start.3
  24.0 0.0 copy-start.4
  24.1 0.6 %shard_map.114 = bf16[240,128]{1,0:T(8,128)(2,1)S(1)} custom-call(s32[1]{0:T(128)} %bitcast.me, bf16[8,5376]{1,0:T(8,128)(2,1)S(1)} %get-tuple-element.11.refs_0_, bf16[8,5376]{1,0:T(8,128)(2,1)S(1)} %collective-permute-done.refs_1_, bf16[8,5376]{1,0:T(8,128)(2,1)S(1)} %collective-permute-done.1.refs_2_, bf16[8,5376]{1,0:T(8,128)(2,1)S(1)} %collective-permute-done.2.refs_3_, ...), custom_call_target="tpu_custom_call" | custom-call | tf_op jit(solution)/shard_map/pallas_call | solution.py:398
  24.7 0.0 copy-start.1
  24.7 16.3 %all_gather.13.gathered = bf16[3840,128]{1,0:T(8,128)(2,1)S(1)} all-gather(bf16[240,128]{1,0:T(8,128)(2,1)S(1)} %shard_map.114), channel_id=1, replica_groups={{0,1,4,5,8,9,12,13,14,15,10,11,6,7,2,3},{16,17,20,21,24,25,28,29,30,31,..., dimensions={0}, use_global_device_ids=true | all-gather | bytes 1044480 | tf_op jit(solution)/shard_map/all_gather | solution.py:403
  41.1 1.5 %shard_map.115 = (bf16[288,128]{1,0:T(8,128)(2,1)S(1)}, bf16[8,3072]{1,0:T(8,128)(2,1)}) custom-call(s32[1]{0:T(128)} %bitcast.me, bf16[3840,128]{1,0:T(8,128)(2,1)S(1)} %all_gather.13.gathered, bf16[8,5376]{1,0:T(8,128)(2,1)S(1)} %get-tuple-element.11.refs_0_, bf16[8,5376]{1,0:T(8,128)(2,1)S(1)} %collective-permute-done.refs_1_, ...), custom_call_target="tpu_custom_call" | custom-call | tf_op jit(solution)/shard_map/pallas_call | solution.py:404
  42.6 6.0 %all-gather = bf16[1152,128]{1,0:T(8,128)(2,1)S(1)} all-gather(bf16[288,128]{1,0:T(8,128)(2,1)S(1)} %get-tuple-element.15), channel_id=2, replica_groups={{0,1,2,3},{4,5,6,7},{8,9,10,11},{12,13,14,15},{16,17,18,19},{20,21,22,2..., dimensions={0}, use_global_device_ids=true | all-gather | bytes 368640 | tf_op jit(solution)/shard_map/all_gather | solution.py:410
  48.6 0.7 %shard_map.116 = (bf16[8,384]{1,0:T(8,128)(2,1)S(1)}, bf16[8,384]{1,0:T(8,128)(2,1)S(1)}, bf16[8,384]{1,0:T(8,128)(2,1)S(1)}, bf16[8,384]{1,0:T(8,128)(2,1)S(1)}) custom-call(s32[1]{0:T(128)} %bitcast.me, bf16[4,288,128]{2,1,0:T(8,128)(2,1)S(1)} %bitcast.8), custom_call_target="tpu_custom_call" | custom-call | tf_op jit(solution)/shard_map/pallas_call | solution.py:412
  49.3 0.5 collective-permute-start.6
  49.8 1.5 %collective-permute-start.7 = (bf16[8,384]{1,0:T(8,128)(2,1)S(1)}, bf16[8,384]{1,0:T(8,128)(2,1)S(1)}, u32[]{:S(2)}, u32[]{:S(2)}) collective-permute-start(bf16[8,384]{1,0:T(8,128)(2,1)S(1)} %get-tuple-element.18), channel_id=1, source_target_pairs={{0,8},{1,9},{2,10},{3,11},{4,12},{5,13},{6,14},{7,15},{8,0},{9,1},... | collective-permute-start | bytes 18440 | tf_op jit(solution)/shard_map/ppermute | solution.py:340
  51.3 2.4 %collective-permute-start.8 = (bf16[8,384]{1,0:T(8,128)(2,1)S(1)}, bf16[8,384]{1,0:T(8,128)(2,1)S(1)}, u32[]{:S(2)}, u32[]{:S(2)}) collective-permute-start(bf16[8,384]{1,0:T(8,128)(2,1)S(1)} %get-tuple-element.19), channel_id=1, source_target_pairs={{0,12},{1,13},{2,14},{3,15},{4,8},{5,9},{6,10},{7,11},{8,4},{9,5},... | collective-permute-start | bytes 18440 | tf_op jit(solution)/shard_map/ppermute | solution.py:340
  53.7 0.6 %collective-permute-done.7.refs_2_ = bf16[8,384]{1,0:T(8,128)(2,1)S(1)} collective-permute-done((bf16[8,384]{1,0:T(8,128)(2,1)S(1)}, bf16[8,384]{1,0:T(8,128)(2,1)S(1)}, u32[]{:S(2)}, u32[]{:S(2)}) %collective-permute-start.7) | collective-permute-done | bytes 6176 | tf_op jit(solution)/shard_map/ppermute | solution.py:340
  54.4 2.4 %collective-permute-done.8.refs_3_ = bf16[8,384]{1,0:T(8,128)(2,1)S(1)} collective-permute-done((bf16[8,384]{1,0:T(8,128)(2,1)S(1)}, bf16[8,384]{1,0:T(8,128)(2,1)S(1)}, u32[]{:S(2)}, u32[]{:S(2)}) %collective-permute-start.8) | collective-permute-done | bytes 6176 | tf_op jit(solution)/shard_map/ppermute | solution.py:340
  56.7 0.6 %shard_map.117 = bf16[8,1536]{1,0:T(8,128)(2,1)} custom-call(s32[1]{0:T(128)} %bitcast.me, bf16[8,384]{1,0:T(8,128)(2,1)S(1)} %get-tuple-element.16.refs_0_, bf16[8,384]{1,0:T(8,128)(2,1)S(1)} %collective-permute-done.6.refs_1_, bf16[8,384]{1,0:T(8,128)(2,1)S(1)} %collective-permute-done.7.refs_2_, bf16[8,384]{1,0:T(8,128)(2,1)S(1)} %collective-permute-done.8.refs_3_), custom_call_target="tpu_custom_call" | custom-call | tf_op jit(solution)/shard_map/pallas_call | solution.py:422
  (13 shorter events, 0.0 us)
Async XLA Ops:
  0.6 23.4 %copy-start = (bf16[3072,192]{0,1:T(8,128)(2,1)S(1)}, bf16[3072,192]{0,1:T(8,128)(2,1)}, u32[]{:S(2)}) copy-start(bf16[3072,192]{0,1:T(8,128)(2,1)} %param.14) | copy-start | bytes 3538948
  1.6 8.3 %collective-permute-start.5 = (bf16[8,5376]{1,0:T(8,128)(2,1)S(1)}, bf16[8,5376]{1,0:T(8,128)(2,1)S(1)}, u32[]{:S(2)}, u32[]{:S(2)}) collective-permute-start(bf16[8,5376]{1,0:T(8,128)(2,1)S(1)} %get-tuple-element.11.refs_0_), channel_id=1, source_target_pairs={{0,12},{1,13},{2,14},{3,15},{4,8},{5,9},{6,10},{7,11},{8,4},{9,5},... | collective-permute-start | bytes 258056 | tf_op jit(solution)/shard_map/ppermute | solution.py:340
  6.8 7.2 %collective-permute-start.4 = (bf16[8,5376]{1,0:T(8,128)(2,1)S(1)}, bf16[8,5376]{1,0:T(8,128)(2,1)S(1)}, u32[]{:S(2)}, u32[]{:S(2)}) collective-permute-start(bf16[8,5376]{1,0:T(8,128)(2,1)S(1)} %get-tuple-element.11.refs_0_), channel_id=1, source_target_pairs={{0,8},{1,9},{2,10},{3,11},{4,12},{5,13},{6,14},{7,15},{8,0},{9,1},... | collective-permute-start | bytes 258056 | tf_op jit(solution)/shard_map/ppermute | solution.py:340
  6.8 7.2 %collective-permute-start.3 = (bf16[8,5376]{1,0:T(8,128)(2,1)S(1)}, bf16[8,5376]{1,0:T(8,128)(2,1)S(1)}, u32[]{:S(2)}, u32[]{:S(2)}) collective-permute-start(bf16[8,5376]{1,0:T(8,128)(2,1)S(1)} %get-tuple-element.11.refs_0_), channel_id=1, source_target_pairs={{0,4},{1,5},{2,6},{3,7},{4,0},{5,1},{6,2},{7,3},{8,12},{9,13},{10,... | collective-permute-start | bytes 258056 | tf_op jit(solution)/shard_map/ppermute | solution.py:340
  7.4 16.6 %collective-permute-start.2 = (bf16[8,5376]{1,0:T(8,128)(2,1)S(1)}, bf16[8,5376]{1,0:T(8,128)(2,1)S(1)}, u32[]{:S(2)}, u32[]{:S(2)}) collective-permute-start(bf16[8,5376]{1,0:T(8,128)(2,1)S(1)} %get-tuple-element.11.refs_0_), channel_id=1, source_target_pairs={{0,3},{1,2},{2,1},{3,0},{4,7},{5,6},{6,5},{7,4},{8,11},{9,10},{10,... | collective-permute-start | bytes 258056 | tf_op jit(solution)/shard_map/ppermute | solution.py:340
  7.8 16.2 %collective-permute-start.1 = (bf16[8,5376]{1,0:T(8,128)(2,1)S(1)}, bf16[8,5376]{1,0:T(8,128)(2,1)S(1)}, u32[]{:S(2)}, u32[]{:S(2)}) collective-permute-start(bf16[8,5376]{1,0:T(8,128)(2,1)S(1)} %get-tuple-element.11.refs_0_), channel_id=1, source_target_pairs={{0,2},{1,3},{2,0},{3,1},{4,6},{5,7},{6,4},{7,5},{8,10},{9,11},{10,... | collective-permute-start | bytes 258056 | tf_op jit(solution)/shard_map/ppermute | solution.py:340
  10.0 14.0 %collective-permute-start = (bf16[8,5376]{1,0:T(8,128)(2,1)S(1)}, bf16[8,5376]{1,0:T(8,128)(2,1)S(1)}, u32[]{:S(2)}, u32[]{:S(2)}) collective-permute-start(bf16[8,5376]{1,0:T(8,128)(2,1)S(1)} %get-tuple-element.11.refs_0_), channel_id=1, source_target_pairs={{0,1},{1,0},{2,3},{3,2},{4,5},{5,4},{6,7},{7,6},{8,9},{9,8},{10,11... | collective-permute-start | bytes 258056 | tf_op jit(solution)/shard_map/ppermute | solution.py:340
  24.0 17.0 %copy-start.2 = (bf16[3072,96]{0,1:T(8,128)(2,1)S(1)}, bf16[3072,96]{0,1:T(8,128)(2,1)}, u32[]{:S(2)}) copy-start(bf16[3072,96]{0,1:T(8,128)(2,1)} %param.18) | copy-start | bytes 1769476
  24.0 17.0 %copy-start.3 = (bf16[3072,96]{0,1:T(8,128)(2,1)S(1)}, bf16[3072,96]{0,1:T(8,128)(2,1)}, u32[]{:S(2)}) copy-start(bf16[3072,96]{0,1:T(8,128)(2,1)} %param.19) | copy-start | bytes 1769476
  24.0 17.0 %copy-start.4 = (f32[2,3072]{1,0:T(2,128)S(1)}, f32[2,3072]{1,0:T(2,128)}, u32[]{:S(2)}) copy-start(f32[2,3072]{1,0:T(2,128)} %refs_5_.1) | copy-start | bytes 73732
  24.7 16.4 %copy-start.1 = (bf16[3072,96]{0,1:T(8,128)(2,1)S(1)}, bf16[3072,96]{0,1:T(8,128)(2,1)}, u32[]{:S(2)}) copy-start(bf16[3072,96]{0,1:T(8,128)(2,1)} %param.17) | copy-start | bytes 1769476
  49.3 4.4 %collective-permute-start.6 = (bf16[8,384]{1,0:T(8,128)(2,1)S(1)}, bf16[8,384]{1,0:T(8,128)(2,1)S(1)}, u32[]{:S(2)}, u32[]{:S(2)}) collective-permute-start(bf16[8,384]{1,0:T(8,128)(2,1)S(1)} %get-tuple-element.17), channel_id=1, source_target_pairs={{0,4},{1,5},{2,6},{3,7},{4,0},{5,1},{6,2},{7,3},{8,12},{9,13},{10,... | collective-permute-start | bytes 18440 | tf_op jit(solution)/shard_map/ppermute | solution.py:340
  49.8 4.5 %collective-permute-start.7 = (bf16[8,384]{1,0:T(8,128)(2,1)S(1)}, bf16[8,384]{1,0:T(8,128)(2,1)S(1)}, u32[]{:S(2)}, u32[]{:S(2)}) collective-permute-start(bf16[8,384]{1,0:T(8,128)(2,1)S(1)} %get-tuple-element.18), channel_id=1, source_target_pairs={{0,8},{1,9},{2,10},{3,11},{4,12},{5,13},{6,14},{7,15},{8,0},{9,1},... | collective-permute-start | bytes 18440 | tf_op jit(solution)/shard_map/ppermute | solution.py:340
  51.3 5.4 %collective-permute-start.8 = (bf16[8,384]{1,0:T(8,128)(2,1)S(1)}, bf16[8,384]{1,0:T(8,128)(2,1)S(1)}, u32[]{:S(2)}, u32[]{:S(2)}) collective-permute-start(bf16[8,384]{1,0:T(8,128)(2,1)S(1)} %get-tuple-element.19), channel_id=1, source_target_pairs={{0,12},{1,13},{2,14},{3,15},{4,8},{5,9},{6,10},{7,11},{8,4},{9,5},... | collective-permute-start | bytes 18440 | tf_op jit(solution)/shard_map/ppermute | solution.py:340
